TPU v7x, 32 devices: a whole 2x2x4 slice. The times are simulated.
32 devices in a mesh: req: 8 (over z, x), head: 4 (over y, core).
Axes of the slice: x: 2, y: 2, z: 4, core: 2. Of those that a mesh axis runs over, the one named last changes fastest.
Arguments:
- resid: bfloat16 [32, 4, 2048], P('req'), may hold values from -6 to 6
- proj: bfloat16 [32, 4, 3, 2048], P('req', None, None, 'head'), may hold values from -6 to 6
- conv_cache: bfloat16 [32, 3, 3, 2048], P('req', None, None, 'head'), may hold values from -6 to 6
- conv_weight: bfloat16 [4, 3, 2048], P(None, None, 'head'), may hold values from -3 to 3
- forget_bias: float32 [2048], P('head'), may hold values from -2 to 6
- owner: int32 [32], replicated, may hold values from 0 to 31, each once
- lengths: int32 [32], replicated, may hold values from 0 to 4096, as said below
- old_state: bfloat16 [32, 16, 128, 128], P('req', 'head'), may hold values from -6 to 6
- norm_gain: float32 [2048], P('head'), may hold values from 0.5 to 1.5
- out_weight: bfloat16 [2048, 2048], P('head'), may hold values from -0.125 to 0.125
Outputs:
- mixed: bfloat16 [32, 4, 2048], P('req')
- new_state: bfloat16 [32, 16, 128, 128], P('req', 'head')
Inputs may be any that keep to these rules, and one draw needn't show every extreme that they name: `lengths`: short requests (below 3) and long ones are mixed; some request has length 0 and some 4096.
All inputs are finite; a program needn't handle non-finite values.
Results may differ from a plain program's by a relative error of at most 0.015.
Values may be sent and summed in bfloat16 or wider, within the bound.
No kernel may reach another device: no remote copies, remote signals or barrier semaphores. Data moves between devices by JAX's collectives and lax.ppermute only.
A program may use at most 64 MiB of HBM per device.

v0:
```python
import jax
import jax.numpy as jnp
from jax import lax
from jax.sharding import PartitionSpec as P


def convolve(proj, conv_cache, conv_weight, lens):
    taps = conv_weight.shape[0]
    new_tokens = proj.shape[1]
    joined = jnp.concatenate([conv_cache, proj], axis=1).astype(jnp.float32)
    places = lens[:, None] + jnp.arange(-(taps - 1), new_tokens, dtype=jnp.int32)[None, :]
    joined = jnp.where((places >= 0)[:, :, None, None], joined, jnp.float32(0.0))
    summed = jnp.zeros(proj.shape, jnp.float32)
    for offset in range(taps):
        begin_at = taps - 1 - offset
        summed = summed + joined[:, begin_at : begin_at + new_tokens] * conv_weight[offset].astype(
            jnp.float32
        )
    return jax.nn.silu(summed).astype(jnp.bfloat16)


def recurrence(convolved, relocated, lens, forget_bias, norm_gain, head_size):
    local_reqs, new_tokens, _, channels = convolved.shape
    head_count = channels // head_size
    values = convolved.astype(jnp.float32).reshape(local_reqs, new_tokens, 3, head_count, head_size)
    queries = values[:, :, 0]
    keep_rate = jax.nn.sigmoid(values[:, :, 1] + forget_bias.reshape(head_count, head_size))
    inputs = values[:, :, 2]
    current = relocated.astype(jnp.float32) * (lens > 0).astype(jnp.float32)[:, None, None, None]
    outputs = []
    for position in range(new_tokens):
        rate_now = keep_rate[:, position]
        current = (
            rate_now[..., None] * current
            + (1.0 - rate_now)[..., None] * inputs[:, position][:, :, None, :]
        )
        outputs.append(jnp.einsum("rhk,rhkv->rhv", queries[:, position], current))
    stacked = jnp.stack(outputs, axis=1)
    inverse_rms = lax.rsqrt(jnp.mean(stacked * stacked, axis=-1, keepdims=True) + 1e-06)
    normed = (stacked * inverse_rms).reshape(local_reqs, new_tokens, channels) * norm_gain
    return (normed.astype(jnp.bfloat16), current.astype(jnp.bfloat16))


def body(
    resid,
    proj,
    conv_cache,
    conv_weight,
    forget_bias,
    owner,
    lengths,
    old_state,
    norm_gain,
    out_weight,
):
    local_reqs = resid.shape[0]
    new_tokens = resid.shape[1]
    devices = lax.axis_size("req")
    own_index = lax.axis_index("req")
    total_reqs = owner.shape[0]
    head_size = old_state.shape[-1]
    inverse = (
        jnp.zeros((total_reqs,), jnp.int32).at[owner].set(jnp.arange(total_reqs, dtype=jnp.int32))
    )
    local_lens = lax.dynamic_slice_in_dim(lengths, own_index * local_reqs, local_reqs)
    convolved = convolve(proj, conv_cache, conv_weight, local_lens)
    pieces = old_state.reshape(local_reqs, devices, -1)
    spread = lax.all_to_all(pieces, "req", split_axis=1, concat_axis=0, tiled=True).reshape(
        total_reqs, -1
    )
    picked = jnp.take(spread, inverse, axis=0).reshape(devices, local_reqs, 1, -1)
    routed = lax.all_to_all(picked, "req", split_axis=0, concat_axis=2, tiled=True)
    relocated = routed.reshape(old_state.shape)
    normed, new_state = recurrence(
        convolved, relocated, local_lens, forget_bias, norm_gain, head_size
    )
    flat_normed = normed.reshape(local_reqs * new_tokens, -1)
    flat_resid = resid.reshape(local_reqs * new_tokens, -1)
    partial_value = jnp.dot(flat_normed, out_weight, preferred_element_type=jnp.float32)
    summed = lax.psum(partial_value, "head")
    mixed = (flat_resid.astype(jnp.float32) + summed).astype(jnp.bfloat16).reshape(resid.shape)
    return (mixed, new_state)


def solution(mesh):
    in_specs = (
        P("req", None, None),
        P("req", None, None, "head"),
        P("req", None, None, "head"),
        P(None, None, "head"),
        P("head"),
        P(),
        P(),
        P("req", "head", None, None),
        P("head"),
        P("head", None),
    )
    out_specs = (P("req", None, None), P("req", "head", None, None))
    return jax.shard_map(body, mesh=mesh, in_specs=in_specs, out_specs=out_specs, check_vma=False)
```

profile of v0, /device:TPU:0, one launch (start us, length us, event | category | flops | bytes accessed | tf_op | source)
XLA Modules:
  0.0 103.1 jit_solution(8104832526261652992)
XLA Ops:
  7.2 0.0 copy-start
  7.2 0.0 copy-start.4
  7.2 0.0 copy-start.3
  7.2 0.0 copy-start.7
  7.2 0.0 copy-start.2
  7.2 0.0 copy-start.8
  7.2 0.0 copy-start.5
  7.2 1.4 %reshape.167 = bf16[4,8,8192]{2,1,0:T(8,128)(2,1)S(1)} reshape(bf16[4,4,128,128]{3,2,1,0:T(8,128)(2,1)} %param.17) | data formatting | bytes 1048576 | tf_op jit(solution)/shard_map/reshape | solution.py:67
  8.6 1.2 %copy.27 = bf16[4,8,8192]{2,0,1:T(4,128)(2,1)} copy(bf16[4,8,8192]{2,1,0:T(8,128)(2,1)S(1)} %reshape.167) | data formatting | bytes 1048576 | tf_op jit(solution)/shard_map/reshape | solution.py:67
  9.8 7.3 %all-to-all-start = ((bf16[4,8,8192]{2,0,1:T(4,128)(2,1)}), bf16[4,8,8192]{2,0,1:T(4,128)(2,1)S(1)}, u32[]{:S(2)}, u32[]{:S(2)}) async-start(bf16[4,8,8192]{2,0,1:T(4,128)(2,1)} %copy.27), calls=%async_computation | async-start | bytes 1048576 | tf_op jit(solution)/shard_map/all_to_all | solution.py:68
  17.1 0.0 copy-done.4
  17.1 0.0 copy-done.3
  17.2 0.0 copy-done.7
  17.2 0.1 compare_convert_fusion
  17.3 0.1 add_compare_fusion
  17.4 0.0 copy-done.2
  17.4 0.1 convert_select_fusion
  17.5 0.1 fusion.21
  17.6 0.0 copy-done.8
  17.7 0.7 scatter_custom_fusion
  18.4 0.1 broadcast_in_dim.46
  18.5 0.0 copy-done.5
  18.6 13.0 %all-to-all-done = bf16[4,8,8192]{2,0,1:T(4,128)(2,1)S(1)} async-done(((bf16[4,8,8192]{2,0,1:T(4,128)(2,1)}), bf16[4,8,8192]{2,0,1:T(4,128)(2,1)S(1)}, u32[]{:S(2)}, u32[]{:S(2)}) %all-to-all-start) | async-done | bytes 524320 | tf_op jit(solution)/shard_map/all_to_all | solution.py:68
  31.6 0.1 reshape.168
  31.7 0.9 gather_fusion
  32.6 0.0 copy-start.1
  32.6 0.2 gather.7
  32.8 1.1 %bitcast_select_fusion = bf16[8,4,1,8192]{3,1,2,0:T(4,128)(2,1)} fusion(bf16[8,4,1,8192]{3,1,0,2:T(4,128)(2,1)S(1)} %gather.7, pred[8,4]{1,0:T(8,128)(4,1)S(1)} %broadcast_in_dim.46), kind=kLoop, calls=%fused_computation.11 | loop fusion | flops 262144 | bytes 1048608 | tf_op jit(solution)/shard_map/jit(_take)/select_n | solution.py:71
  33.9 3.6 %all-to-all-start.1 = ((bf16[8,4,1,8192]{3,1,2,0:T(4,128)(2,1)}), bf16[8,4,1,8192]{3,1,2,0:T(4,128)(2,1)S(1)}, u32[]{:S(2)}, u32[]{:S(2)}) async-start(bf16[8,4,1,8192]{3,1,2,0:T(4,128)(2,1)} %bitcast_select_fusion), calls=%async_computation.1 | async-start | bytes 1048576 | tf_op jit(solution)/shard_map/all_to_all | solution.py:72
  37.5 0.0 all-reduce.2.cloned.1.call-start
  37.6 0.0 copy-done.1
  37.7 14.5 %all-to-all-done.1 = bf16[8,4,1,8192]{3,1,2,0:T(4,128)(2,1)S(1)} async-done(((bf16[8,4,1,8192]{3,1,2,0:T(4,128)(2,1)}), bf16[8,4,1,8192]{3,1,2,0:T(4,128)(2,1)S(1)}, u32[]{:S(2)}, u32[]{:S(2)}) %all-to-all-start.1) | async-done | bytes 524320 | tf_op jit(solution)/shard_map/all_to_all | solution.py:72
  52.2 0.1 convert_bitcast_fusion
  52.3 1.6 %copy.29 = f32[1,4,8,1,8192]{4,2,1,3,0:T(8,128)} copy(f32[1,4,8,1,8192]{4,1,2,3,0:T(4,128)S(1)} %convert_bitcast_fusion) | data formatting | bytes 2097152 | tf_op jit(solution)/shard_map/convert_element_type | solution.py:29
  53.9 1.4 %reshape.175 = f32[4,4,128,128]{3,2,1,0:T(8,128)S(1)} reshape(f32[1,4,8,1,8192]{4,2,1,3,0:T(8,128)} %copy.29) | data formatting | bytes 2097152 | tf_op jit(solution)/shard_map/convert_element_type | solution.py:29
  55.2 0.7 fusion.3
  56.0 1.5 %fusion = f32[4,4,1,128]{3,2,1,0:T(1,128)S(1)} fusion(f32[4,4,128,128]{3,2,1,0:T(8,128)S(1)} %reshape.175, f32[4,4,128]{2,1,0:T(4,128)S(1)} %get-tuple-element.15, f32[4,4,128]{2,1,0:T(4,128)S(1)} %get-tuple-element.11, f32[4,4,128]{2,1,0:T(4,128)S(1)} %get-tuple-element.7, f32[4,4,128]{2,1,0:T(4,128)S(1)} %get-tuple-element.12, ...), kind=kOutput, calls=%fused_computation.7 | convolution fusion | flops 2359296 | bytes 1110032 | tf_op jit(solution)/shard_map/rhk,rhkv->rhv/dot_general | solution.py:37
  57.4 2.4 %fusion.34 = f32[4,4,1,128]{3,2,1,0:T(1,128)S(1)} fusion(bf16[4,4,128,1]{2,1,0,3:T(4,128)(2,1)S(1)} %get-tuple-element.18, f32[4,4,128,128]{3,2,1,0:T(8,128)S(1)} %reshape.175, f32[4,4,128]{2,1,0:T(4,128)S(1)} %get-tuple-element.14, f32[4,4,128]{2,1,0:T(4,128)S(1)} %get-tuple-element.10, f32[4,4,128]{2,1,0:T(4,128)S(1)} %get-tuple-element.6, ...), kind=kOutput, calls=%fused_computation.67 | convolution fusion | flops 3145728 | bytes 1134608 | tf_op jit(solution)/shard_map/rhk,rhkv->rhv/dot_general | solution.py:37
  59.8 0.0 copy-start.6
  59.8 2.9 %fusion.2 = f32[4,4,1,128]{3,2,1,0:T(1,128)S(1)} fusion(f32[4,4,128]{2,1,0:T(4,128)S(1)} %get-tuple-element.13, f32[4,4,128]{2,1,0:T(4,128)S(1)} %get-tuple-element.9, f32[4,4,128]{2,1,0:T(4,128)S(1)} %get-tuple-element.5, bf16[4,4,128,1]{2,1,0,3:T(4,128)(2,1)S(1)} %get-tuple-element.17, f32[4,4,128,128]{3,2,1,0:T(8,128)S(1)} %reshape.175, ...), kind=kOutput, calls=%fused_computation.9 | convolution fusion | flops 3932160 | bytes 1159184 | tf_op jit(solution)/shard_map/rhk,rhkv->rhv/dot_general | solution.py:37
  62.7 0.1 fusion.29
  62.9 0.1 mul.212
  63.0 0.0 copy-done
  63.0 0.0 copy-done.6
  63.0 1.0 %fusion.30 = f32[16,2048]{1,0:T(8,128)} fusion(bf16[512,2048]{1,0:T(8,128)(2,1)S(1)} %copy-done, f32[16,512]{1,0:T(8,128)S(1)} %stack.32, f32[2,8,4,128]{3,2,1,0:T(4,128)S(1)} %bitcast.112, f32[512]{0:T(512)S(1)} %copy-done.6), kind=kOutput, calls=%fused_computation.51 | convolution fusion | flops 33579008 | bytes 2295808 | tf_op jit(solution)/shard_map/dot_general | solution.py:79
  64.0 0.0 all-reduce.2.cloned.1.call-update
  64.1 3.2 %fusion.1 = bf16[4,4,128,128]{3,2,1,0:T(8,128)(2,1)} fusion(f32[4,4,128]{2,1,0:T(4,128)S(1)} %get-tuple-element.13, f32[4,4,128]{2,1,0:T(4,128)S(1)} %get-tuple-element.9, f32[4,4,128]{2,1,0:T(4,128)S(1)} %get-tuple-element.5, f32[4,4,128]{2,1,0:T(4,128)S(1)} %get-tuple-element.14, f32[4,4,128]{2,1,0:T(4,128)S(1)} %get-tuple-element.10, ...), kind=kLoop, calls=%fused_computation.8 | loop fusion | flops 3670016 | bytes 1671184 | tf_op jit(solution)/shard_map/convert_element_type | solution.py:41
  67.3 27.5 %all-reduce.2.cloned.1.call-done = f32[16,2048]{1,0:T(8,128)} async-done(((f32[16,2048]{1,0:T(8,128)}), f32[16,2048]{1,0:T(8,128)}) %all-reduce.2.cloned.1.call-update) | async-done | bytes 131088 | tf_op jit(solution)/shard_map/psum | solution.py:80
  94.7 0.9 add_convert_fusion
  95.6 0.7 reshape.169
  (24 shorter events, 0.3 us)
Async XLA Ops:
  7.2 55.8 %copy-start = (bf16[512,2048]{1,0:T(8,128)(2,1)S(1)}, bf16[512,2048]{1,0:T(8,128)(2,1)}, u32[]{:S(2)}) copy-start(bf16[512,2048]{1,0:T(8,128)(2,1)} %param.19) | copy-start | bytes 6291460
  7.2 9.9 %copy-start.4 = (bf16[4,3,3,512]{3,0,2,1:T(4,128)(2,1)S(1)}, bf16[4,3,3,512]{3,0,2,1:T(4,128)(2,1)}, u32[]{:S(2)}) copy-start(bf16[4,3,3,512]{3,0,2,1:T(4,128)(2,1)} %param.12) | copy-start | bytes 110596
  7.2 10.0 %copy-start.3 = (bf16[4,3,512]{2,0,1:T(4,128)(2,1)S(1)}, bf16[4,3,512]{2,0,1:T(4,128)(2,1)}, u32[]{:S(2)}) copy-start(bf16[4,3,512]{2,0,1:T(4,128)(2,1)} %param.13) | copy-start | bytes 36868
  7.2 10.0 %copy-start.7 = (s32[32]{0:T(128)S(1)}, s32[32]{0:T(128)}, u32[]{:S(2)}) copy-start(s32[32]{0:T(128)} %param.16) | copy-start | bytes 388
  7.2 10.2 %copy-start.2 = (bf16[4,4,3,512]{3,1,2,0:T(4,128)(2,1)S(1)}, bf16[4,4,3,512]{3,1,2,0:T(4,128)(2,1)}, u32[]{:S(2)}) copy-start(bf16[4,4,3,512]{3,1,2,0:T(4,128)(2,1)} %param.11) | copy-start | bytes 147460
  7.2 10.4 %copy-start.8 = (s32[32]{0:T(128)S(1)}, s32[32]{0:T(128)}, u32[]{:S(2)}) copy-start(s32[32]{0:T(128)} %param.15) | copy-start | bytes 388
  7.2 11.3 %copy-start.5 = (f32[512]{0:T(512)S(1)}, f32[512]{0:T(512)}, u32[]{:S(2)}) copy-start(f32[512]{0:T(512)} %param.14) | copy-start | bytes 6148
  9.8 21.7 %all-to-all-start = ((bf16[4,8,8192]{2,0,1:T(4,128)(2,1)}), bf16[4,8,8192]{2,0,1:T(4,128)(2,1)S(1)}, u32[]{:S(2)}, u32[]{:S(2)}) async-start(bf16[4,8,8192]{2,0,1:T(4,128)(2,1)} %copy.27), calls=%async_computation | async-start | bytes 1048576 | tf_op jit(solution)/shard_map/all_to_all | solution.py:68
  32.6 5.0 %copy-start.1 = (bf16[4,4,2048]{2,1,0:T(4,128)(2,1)S(1)}, bf16[4,4,2048]{2,1,0:T(4,128)(2,1)}, u32[]{:S(2)}) copy-start(bf16[4,4,2048]{2,1,0:T(4,128)(2,1)} %param.10) | copy-start | bytes 196612
  33.9 18.3 %all-to-all-start.1 = ((bf16[8,4,1,8192]{3,1,2,0:T(4,128)(2,1)}), bf16[8,4,1,8192]{3,1,2,0:T(4,128)(2,1)S(1)}, u32[]{:S(2)}, u32[]{:S(2)}) async-start(bf16[8,4,1,8192]{3,1,2,0:T(4,128)(2,1)} %bitcast_select_fusion), calls=%async_computation.1 | async-start | bytes 1048576 | tf_op jit(solution)/shard_map/all_to_all | solution.py:72
  37.5 57.2 %all-reduce.2.cloned.1.call-start = ((), (), s32[]{:S(2)}) async-start(), calls=%async_computation.2 | async-start | bytes 262144 | tf_op jit(solution)/shard_map/psum | solution.py:80
  59.8 3.2 %copy-start.6 = (f32[512]{0:T(512)S(1)}, f32[512]{0:T(512)}, u32[]{:S(2)}) copy-start(f32[512]{0:T(512)} %param.18) | copy-start | bytes 6148
Sparse Core Ops, SparseCore 0:
  64.2 30.4 all-reduce.1
where the time goes:
time: 103 us
  waiting for transfers between devices  55 us (53%)
  between operations  14.4 us (14%)
  starting transfers between devices  10.9 us (11%)
  matrix products  8.49 us (8%)
  local copies, waits for them, and re-layouts  8.43 us (8%)
  other arithmetic  5.91 us (6%)
    psum x1, waiting for transfers between devices, body(): summed = lax.psum(partial_value, 'head')  27.5 us
    all_to_all x1, waiting for transfers between devices, body(): lax.all_to_all(picked, 'req', split_axis=0, concat_axis=2, tiled=True)  14.5 us
    all_to_all x1, waiting for transfers between devices, body(): lax.all_to_all(pieces, 'req', split_axis=1, concat_axis=0, tiled=True)  13 us
    dot_general x4, matrix products, recurrence(): outputs.append(jnp.einsum('rhk,rhkv->rhv', queries[:, position], current))  7.46 us
    all_to_all x1, starting transfers between devices, body(): lax.all_to_all(pieces, 'req', split_axis=1, concat_axis=0, tiled=True)  7.25 us
    all_to_all x1, starting transfers between devices, body(): lax.all_to_all(picked, 'req', split_axis=0, concat_axis=2, tiled=True)  3.64 us
    convert_element_type x1, other arithmetic, recurrence(): return (normed.astype(jnp.bfloat16), current.astype(jnp.bfloat16))  3.19 us
    convert_element_type x2, local copies, waits for them, and re-layouts, recurrence(): relocated.astype(jnp.float32)  2.97 us
  transfers between devices with their start and end apart: 3, of which 3 were waited for; matrix products, arithmetic and copies ran while one was open for 4% of the time, Pallas kernels for 0%

commit v1 on v0

--- a/solution.py
+++ b/solution.py
@@ -2,6 +2,7 @@
 import jax.numpy as jnp
 from jax import lax
 from jax.sharding import PartitionSpec as P
+from jax.lax import all_gather
 
 
 def convolve(proj, conv_cache, conv_weight, lens):
@@ -77,7 +78,8 @@
     flat_normed = normed.reshape(local_reqs * new_tokens, -1)
     flat_resid = resid.reshape(local_reqs * new_tokens, -1)
     partial_value = jnp.dot(flat_normed, out_weight, preferred_element_type=jnp.float32)
-    summed = lax.psum(partial_value, "head")
+    threads_step_on = lambda s0, along_axis: jnp.sum(all_gather(s0, along_axis), 0)
+    summed = threads_step_on(partial_value, "head")
     mixed = (flat_resid.astype(jnp.float32) + summed).astype(jnp.bfloat16).reshape(resid.shape)
     return (mixed, new_state)
 

time: 103 us -> 68.3 us (0.66)
  waiting for transfers between devices: 55 us -> 27.6 us
  between operations: 14.4 us -> 0.98 us
  blocking collectives: 0 us -> 7.19 us
    psum x1 -> x0, waiting for transfers between devices: 27.5 us -> none  [body(): summed = lax.psum(partial_value, 'head')]
    all_gather x0 -> x1, blocking collectives: none -> 7.19 us  [body(): all_gather(s0, along_axis)]
  transfers between devices with their start and end apart: 3 -> 2, of which waited for: 3 -> 2; matrix products, arithmetic and copies ran while one was open for 4% -> 2% of each run, Pallas kernels for 0% -> 0%
where the time goes in v1:
time: 68.3 us; the launch traced here: 68 us
  waiting for transfers between devices  27.6 us (40%)
  starting transfers between devices  10.9 us (16%)
  matrix products  7.84 us (11%)
  local copies, waits for them, and re-layouts  7.78 us (11%)
  blocking collectives  7.19 us (11%)
  other arithmetic  5.67 us (8%)
  between operations  0.98 us (1%)
    all_to_all x1, waiting for transfers between devices, body(): lax.all_to_all(picked, 'req', split_axis=0, concat_axis=2, tiled=True)  14.6 us
    all_to_all x1, waiting for transfers between devices, body(): lax.all_to_all(pieces, 'req', split_axis=1, concat_axis=0, tiled=True)  13 us
    dot_general x4, matrix products, recurrence(): outputs.append(jnp.einsum('rhk,rhkv->rhv', queries[:, position], current))  7.46 us
    all_to_all x1, starting transfers between devices, body(): lax.all_to_all(pieces, 'req', split_axis=1, concat_axis=0, tiled=True)  7.25 us
    all_gather x1, blocking collectives, body(): all_gather(s0, along_axis)  7.19 us
    all_to_all x1, starting transfers between devices, body(): lax.all_to_all(picked, 'req', split_axis=0, concat_axis=2, tiled=True)  3.64 us
    convert_element_type x1, other arithmetic, recurrence(): return (normed.astype(jnp.bfloat16), current.astype(jnp.bfloat16))  3.19 us
    convert_element_type x2, local copies, waits for them, and re-layouts, recurrence(): relocated.astype(jnp.float32)  2.97 us
  transfers between devices with their start and end apart: 2, of which 2 were waited for; matrix products, arithmetic and copies ran while one was open for 2% of the time, Pallas kernels for 0%

profile of v1, /device:TPU:0, one launch (start us, length us, event | category | flops | bytes accessed | tf_op | source)
XLA Modules:
  0.0 68.0 jit_solution(1179416869927369285)
XLA Ops:
  0.6 0.0 copy-start
  0.6 0.0 copy-start.8
  0.7 0.0 copy-start.3
  0.7 0.0 copy-start.4
  0.7 0.0 copy-start.7
  0.7 0.0 copy-start.2
  0.7 0.0 copy-start.5
  0.7 1.4 %reshape.164 = bf16[4,8,8192]{2,1,0:T(8,128)(2,1)S(1)} reshape(bf16[4,4,128,128]{3,2,1,0:T(8,128)(2,1)} %param.17) | data formatting | bytes 1048576 | tf_op jit(solution)/shard_map/reshape | solution.py:68
  2.1 1.2 %copy.27 = bf16[4,8,8192]{2,0,1:T(4,128)(2,1)} copy(bf16[4,8,8192]{2,1,0:T(8,128)(2,1)S(1)} %reshape.164) | data formatting | bytes 1048576 | tf_op jit(solution)/shard_map/reshape | solution.py:68
  3.3 7.3 %all-to-all-start = ((bf16[4,8,8192]{2,0,1:T(4,128)(2,1)}), bf16[4,8,8192]{2,0,1:T(4,128)(2,1)S(1)}, u32[]{:S(2)}, u32[]{:S(2)}) async-start(bf16[4,8,8192]{2,0,1:T(4,128)(2,1)} %copy.27), calls=%async_computation | async-start | bytes 1048576 | tf_op jit(solution)/shard_map/all_to_all | solution.py:69
  10.6 0.0 copy-done.8
  10.6 0.7 scatter_custom_fusion
  11.3 0.1 broadcast_in_dim.46
  11.4 0.0 copy-done.3
  11.4 0.0 copy-done.4
  11.5 0.0 copy-done.7
  11.5 0.1 compare_convert_fusion
  11.6 0.1 add_compare_fusion
  11.6 0.0 copy-done.2
  11.7 0.1 convert_select_fusion
  11.7 0.1 fusion.21
  12.0 0.0 copy-done.5
  12.0 13.0 %all-to-all-done = bf16[4,8,8192]{2,0,1:T(4,128)(2,1)S(1)} async-done(((bf16[4,8,8192]{2,0,1:T(4,128)(2,1)}), bf16[4,8,8192]{2,0,1:T(4,128)(2,1)S(1)}, u32[]{:S(2)}, u32[]{:S(2)}) %all-to-all-start) | async-done | bytes 524320 | tf_op jit(solution)/shard_map/all_to_all | solution.py:69
  25.1 0.1 reshape.165
  25.2 0.9 %gather_fusion = bf16[32,8192]{1,0:T(8,128)(2,1)S(1)} fusion(bf16[32,8192]{1,0:T(8,128)(2,1)S(1)} %reshape.165, s32[1024]{0:T(1024)S(1)} %pad_clamp_fusion), kind=kCustom, calls=%fused_computation | custom fusion | bytes 1048704 | tf_op jit(solution)/shard_map/jit(_take)/gather | solution.py:72
  26.1 0.2 gather.7
  26.3 1.1 %bitcast_select_fusion = bf16[8,4,1,8192]{3,1,2,0:T(4,128)(2,1)} fusion(bf16[8,4,1,8192]{3,1,0,2:T(4,128)(2,1)S(1)} %gather.7, pred[8,4]{1,0:T(8,128)(4,1)S(1)} %broadcast_in_dim.46), kind=kLoop, calls=%fused_computation.11 | loop fusion | flops 262144 | bytes 1048608 | tf_op jit(solution)/shard_map/jit(_take)/select_n | solution.py:72
  27.4 3.6 %all-to-all-start.1 = ((bf16[8,4,1,8192]{3,1,2,0:T(4,128)(2,1)}), bf16[8,4,1,8192]{3,1,2,0:T(4,128)(2,1)S(1)}, u32[]{:S(2)}, u32[]{:S(2)}) async-start(bf16[8,4,1,8192]{3,1,2,0:T(4,128)(2,1)} %bitcast_select_fusion), calls=%async_computation.1 | async-start | bytes 1048576 | tf_op jit(solution)/shard_map/all_to_all | solution.py:73
  31.1 14.6 %all-to-all-done.1 = bf16[8,4,1,8192]{3,1,2,0:T(4,128)(2,1)S(1)} async-done(((bf16[8,4,1,8192]{3,1,2,0:T(4,128)(2,1)}), bf16[8,4,1,8192]{3,1,2,0:T(4,128)(2,1)S(1)}, u32[]{:S(2)}, u32[]{:S(2)}) %all-to-all-start.1) | async-done | bytes 524320 | tf_op jit(solution)/shard_map/all_to_all | solution.py:73
  45.7 0.1 convert_bitcast_fusion
  45.7 1.6 %copy.29 = f32[1,4,8,1,8192]{4,2,1,3,0:T(8,128)} copy(f32[1,4,8,1,8192]{4,1,2,3,0:T(4,128)S(1)} %convert_bitcast_fusion) | data formatting | bytes 2097152 | tf_op jit(solution)/shard_map/convert_element_type | solution.py:30
  47.3 1.4 %reshape.170 = f32[4,4,128,128]{3,2,1,0:T(8,128)S(1)} reshape(f32[1,4,8,1,8192]{4,2,1,3,0:T(8,128)} %copy.29) | data formatting | bytes 2097152 | tf_op jit(solution)/shard_map/convert_element_type | solution.py:30
  48.7 3.2 %fusion.1 = bf16[4,4,128,128]{3,2,1,0:T(8,128)(2,1)} fusion(f32[4,4,128]{2,1,0:T(4,128)S(1)} %get-tuple-element.13, f32[4,4,128]{2,1,0:T(4,128)S(1)} %get-tuple-element.9, f32[4,4,128]{2,1,0:T(4,128)S(1)} %get-tuple-element.5, f32[4,4,128]{2,1,0:T(4,128)S(1)} %get-tuple-element.14, f32[4,4,128]{2,1,0:T(4,128)S(1)} %get-tuple-element.10, ...), kind=kLoop, calls=%fused_computation.8 | loop fusion | flops 3670016 | bytes 1671184 | tf_op jit(solution)/shard_map/convert_element_type | solution.py:42
  51.9 2.9 %fusion.2 = f32[4,4,1,128]{3,2,1,0:T(1,128)S(1)} fusion(f32[4,4,128]{2,1,0:T(4,128)S(1)} %get-tuple-element.13, f32[4,4,128]{2,1,0:T(4,128)S(1)} %get-tuple-element.9, f32[4,4,128]{2,1,0:T(4,128)S(1)} %get-tuple-element.5, bf16[4,4,128,1]{2,1,0,3:T(4,128)(2,1)S(1)} %get-tuple-element.17, f32[4,4,128,128]{3,2,1,0:T(8,128)S(1)} %reshape.170, ...), kind=kOutput, calls=%fused_computation.9 | convolution fusion | flops 3932160 | bytes 1159184 | tf_op jit(solution)/shard_map/rhk,rhkv->rhv/dot_general | solution.py:38
  54.8 1.5 %fusion = f32[4,4,1,128]{3,2,1,0:T(1,128)S(1)} fusion(f32[4,4,128,128]{3,2,1,0:T(8,128)S(1)} %reshape.170, f32[4,4,128]{2,1,0:T(4,128)S(1)} %get-tuple-element.15, f32[4,4,128]{2,1,0:T(4,128)S(1)} %get-tuple-element.11, f32[4,4,128]{2,1,0:T(4,128)S(1)} %get-tuple-element.7, f32[4,4,128]{2,1,0:T(4,128)S(1)} %get-tuple-element.12, ...), kind=kOutput, calls=%fused_computation.7 | convolution fusion | flops 2359296 | bytes 1110032 | tf_op jit(solution)/shard_map/rhk,rhkv->rhv/dot_general | solution.py:38
  56.2 0.0 copy-start.6
  56.3 2.4 %fusion.34 = f32[4,4,1,128]{3,2,1,0:T(1,128)S(1)} fusion(bf16[4,4,128,1]{2,1,0,3:T(4,128)(2,1)S(1)} %get-tuple-element.18, f32[4,4,128,128]{3,2,1,0:T(8,128)S(1)} %reshape.170, f32[4,4,128]{2,1,0:T(4,128)S(1)} %get-tuple-element.14, f32[4,4,128]{2,1,0:T(4,128)S(1)} %get-tuple-element.10, f32[4,4,128]{2,1,0:T(4,128)S(1)} %get-tuple-element.6, ...), kind=kOutput, calls=%fused_computation.67 | convolution fusion | flops 3145728 | bytes 1134608 | tf_op jit(solution)/shard_map/rhk,rhkv->rhv/dot_general | solution.py:38
  58.6 0.7 %fusion.3 = f32[4,4,1,128]{3,2,1,0:T(1,128)S(1)} fusion(f32[4,4,128,128]{3,2,1,0:T(8,128)S(1)} %reshape.170, f32[4,4,128]{2,1,0:T(4,128)S(1)} %get-tuple-element.12, f32[4,4,128]{2,1,0:T(4,128)S(1)} %get-tuple-element.8, f32[4]{0:T(128)S(1)} %get-tuple-element.2, f32[4,4,128]{2,1,0:T(4,128)S(1)} %get-tuple-element.4, ...), kind=kOutput, calls=%fused_computation.10 | convolution fusion | flops 1572864 | bytes 1085456 | tf_op jit(solution)/shard_map/rhk,rhkv->rhv/dot_general | solution.py:38
  59.4 0.0 copy-start.1
  59.4 0.1 fusion.29
  59.6 0.1 mul.212
  59.6 0.0 copy-done
  59.6 0.0 copy-done.6
  59.7 0.4 fusion.30
  60.0 7.2 %all-gather = f32[64,2048]{1,0:T(8,128)S(1)} all-gather(f32[16,2048]{1,0:T(8,128)S(1)} %fusion.30), channel_id=2, replica_groups=mesh['req'=8,'head'=4] {'head'}, dimensions={0}, use_global_device_ids=true | all-gather | bytes 655360 | tf_op jit(solution)/shard_map/all_gather | solution.py:81
  67.3 0.0 copy-done.1
  67.3 0.7 add_convert_fusion
  (25 shorter events, 0.3 us)
Async XLA Ops:
  0.6 59.0 %copy-start = (bf16[512,2048]{1,0:T(8,128)(2,1)S(1)}, bf16[512,2048]{1,0:T(8,128)(2,1)}, u32[]{:S(2)}) copy-start(bf16[512,2048]{1,0:T(8,128)(2,1)} %param.19) | copy-start | bytes 6291460
  0.6 9.9 %copy-start.8 = (s32[32]{0:T(128)S(1)}, s32[32]{0:T(128)}, u32[]{:S(2)}) copy-start(s32[32]{0:T(128)} %param.15) | copy-start | bytes 388
  0.7 10.7 %copy-start.3 = (bf16[4,3,512]{2,0,1:T(4,128)(2,1)S(1)}, bf16[4,3,512]{2,0,1:T(4,128)(2,1)}, u32[]{:S(2)}) copy-start(bf16[4,3,512]{2,0,1:T(4,128)(2,1)} %param.13) | copy-start | bytes 36868
  0.7 10.8 %copy-start.4 = (bf16[4,3,3,512]{3,0,2,1:T(4,128)(2,1)S(1)}, bf16[4,3,3,512]{3,0,2,1:T(4,128)(2,1)}, u32[]{:S(2)}) copy-start(bf16[4,3,3,512]{3,0,2,1:T(4,128)(2,1)} %param.12) | copy-start | bytes 110596
  0.7 10.8 %copy-start.7 = (s32[32]{0:T(128)S(1)}, s32[32]{0:T(128)}, u32[]{:S(2)}) copy-start(s32[32]{0:T(128)} %param.16) | copy-start | bytes 388
  0.7 11.0 %copy-start.2 = (bf16[4,4,3,512]{3,1,2,0:T(4,128)(2,1)S(1)}, bf16[4,4,3,512]{3,1,2,0:T(4,128)(2,1)}, u32[]{:S(2)}) copy-start(bf16[4,4,3,512]{3,1,2,0:T(4,128)(2,1)} %param.11) | copy-start | bytes 147460
  0.7 11.3 %copy-start.5 = (f32[512]{0:T(512)S(1)}, f32[512]{0:T(512)}, u32[]{:S(2)}) copy-start(f32[512]{0:T(512)} %param.14) | copy-start | bytes 6148
  3.3 21.7 %all-to-all-start = ((bf16[4,8,8192]{2,0,1:T(4,128)(2,1)}), bf16[4,8,8192]{2,0,1:T(4,128)(2,1)S(1)}, u32[]{:S(2)}, u32[]{:S(2)}) async-start(bf16[4,8,8192]{2,0,1:T(4,128)(2,1)} %copy.27), calls=%async_computation | async-start | bytes 1048576 | tf_op jit(solution)/shard_map/all_to_all | solution.py:69
  27.4 18.3 %all-to-all-start.1 = ((bf16[8,4,1,8192]{3,1,2,0:T(4,128)(2,1)}), bf16[8,4,1,8192]{3,1,2,0:T(4,128)(2,1)S(1)}, u32[]{:S(2)}, u32[]{:S(2)}) async-start(bf16[8,4,1,8192]{3,1,2,0:T(4,128)(2,1)} %bitcast_select_fusion), calls=%async_computation.1 | async-start | bytes 1048576 | tf_op jit(solution)/shard_map/all_to_all | solution.py:73
  56.2 3.4 %copy-start.6 = (f32[512]{0:T(512)S(1)}, f32[512]{0:T(512)}, u32[]{:S(2)}) copy-start(f32[512]{0:T(512)} %param.18) | copy-start | bytes 6148
  59.4 8.0 %copy-start.1 = (bf16[4,4,2048]{2,1,0:T(4,128)(2,1)S(1)}, bf16[4,4,2048]{2,1,0:T(4,128)(2,1)}, u32[]{:S(2)}) copy-start(bf16[4,4,2048]{2,1,0:T(4,128)(2,1)} %param.10) | copy-start | bytes 196612
